TPU v7x, 32 devices: a whole 2x2x4 slice. The times are simulated.
32 devices in a mesh: dp: 8 (over y, x, core), mp: 4 (over z).
Axes of the slice: x: 2, y: 2, z: 4, core: 2. Of those that a mesh axis runs over, the one named last changes fastest.
Arguments:
- gen_rows: bfloat16 [1024, 5120], P(('dp', 'mp')), may hold values from -6 to 6
- lengths: int32 [32, 4], P('dp'), may hold values from 1 to 16, 32 in all within a row
- assign: int32 [32, 4], P('dp'), may hold values from 0 to 3, each once within a row
- rewards: float32 [32, 4], P('dp'), may hold values from 0 to 1
- upstream: bfloat16 [2048, 2048], P('dp', 'mp'), may hold values from -6 to 6
- weight: bfloat16 [5120, 2048], P(None, 'mp'), may hold values from -0.078125 to 0.078125
- q_init: float32 [2048, 64], P('mp'), may hold values from -6 to 6
- resid: float32 [32, 128, 2048], P('dp', None, 'mp'), may hold values from -4 to 4
- block_ids: int32 [32], P('dp'), may hold values from 0 to 39, as said below
Outputs:
- p_factor: float32 [5120, 256], P(None, 'mp')
- q_factor: float32 [2048, 64], P('mp')
- resid_out: float32 [32, 128, 2048], P('dp', None, 'mp')
Inputs may be any that keep to these rules, and one draw needn't show every extreme that they name: Each row holds the lengths of one generator's 4 sequences; they sum to 32. `assign`: each row names every learner once. `block_ids`: the 4 ids of one replica are distinct.
All inputs are finite; a program needn't handle non-finite values.
Results may differ from a plain program's by a relative error of at most 0.003.
Values may be sent and summed in bfloat16 or wider, within the bound.
No kernel may reach another device: no remote copies, remote signals or barrier semaphores. Data moves between devices by JAX's collectives and lax.ppermute only.
A program may use at most 64 MiB of HBM per device.

v0:
```python
import jax
import jax.numpy as jnp
from jax import lax
from jax.sharding import PartitionSpec as P

HIGHEST_PRECISION = lax.Precision.HIGHEST


def packed_tables(lengths, assign, rewards, slot_count, capacity):
    groups, sequences = lengths.shape
    offsets = jnp.cumsum(lengths, axis=1) - lengths
    advantage = rewards - jnp.mean(rewards, axis=1, keepdims=True)
    seq_weight = advantage / lengths.astype(rewards.dtype)
    positions = jnp.arange(slot_count)
    seq_index = jnp.arange(sequences)
    inside = (offsets[:, None, :] <= positions[None, :, None]).astype(jnp.int32)
    owner = jnp.sum(inside, axis=2) - 1
    picked = owner[:, :, None] == seq_index[None, None, :]
    seq_start = jnp.sum(jnp.where(picked, offsets[:, None, :], 0), axis=2)
    learner = jnp.sum(jnp.where(picked, assign[:, None, :], 0), axis=2)
    row_weight = jnp.sum(jnp.where(picked, seq_weight[:, None, :], 0.0), axis=2)
    source = jnp.arange(groups)[:, None]
    slot_table = learner * (groups * capacity) + source * capacity + positions[None, :] - seq_start
    return (slot_table, row_weight)


def row_gradient(row_block, upstream_rows, weights_here, weight):
    hidden = jnp.dot(row_block, weight, preferred_element_type=jnp.float32)
    tangent = jnp.tanh(hidden)
    grad_h = (
        weights_here[:, None] * upstream_rows.astype(jnp.float32) * (1.0 - tangent * tangent)
    ).astype(jnp.bfloat16)
    return jnp.einsum("nd,nc->dc", row_block, grad_h, preferred_element_type=jnp.float32)


def shards(gen_rows, lengths, assign, rewards, upstream, weight, q_init, resid, block_ids):
    groups = lax.axis_size("mp")
    slot_count = gen_rows.shape[0]
    capacity = upstream.shape[0] // (groups * groups)
    slot_table, row_weight = packed_tables(lengths, assign, rewards, slot_count, capacity)
    flat_slot = slot_table.reshape(-1)
    flat_weight = row_weight.reshape(-1)
    upstream_rows = jnp.take(upstream, flat_slot, axis=0)
    gradient = row_gradient(
        lax.all_gather(gen_rows, "mp", axis=0, tiled=True), upstream_rows, flat_weight, weight
    )
    block_rows = resid.shape[1]
    for block in range(resid.shape[0]):
        first_row = block_ids[block] * block_rows
        current = lax.dynamic_slice_in_dim(gradient, first_row, block_rows, 0)
        gradient = lax.dynamic_update_slice_in_dim(gradient, current + resid[block], first_row, 0)
    p_local = jnp.dot(gradient, q_init, precision=HIGHEST_PRECISION)
    p_sum = lax.psum(p_local, "dp")
    gram_matrix = jnp.einsum("dr,ds->rs", p_sum, p_sum, precision=HIGHEST_PRECISION)
    factor_low = jnp.linalg.cholesky(gram_matrix)
    p_factor = jax.scipy.linalg.solve_triangular(factor_low, p_sum.T, lower=True).T
    q_local = jnp.einsum("dc,dr->cr", gradient, p_factor, precision=HIGHEST_PRECISION)
    q_factor = lax.psum(q_local, "dp") / lax.axis_size("dp")
    new_blocks = []
    for block in range(resid.shape[0]):
        first_row = block_ids[block] * block_rows
        merged_rows = lax.dynamic_slice_in_dim(gradient, first_row, block_rows, 0)
        p_rows = lax.dynamic_slice_in_dim(p_factor, first_row, block_rows, 0)
        approx = jnp.einsum("br,cr->bc", p_rows, q_factor, precision=HIGHEST_PRECISION)
        new_blocks.append(merged_rows - approx)
    return (p_factor, q_factor, jnp.stack(new_blocks))


def solution(mesh):
    placed = (
        P(("dp", "mp"), None),
        P("dp", None),
        P("dp", None),
        P("dp", None),
        P("dp", "mp"),
        P(None, "mp"),
        P("mp", None),
        P("dp", None, "mp"),
        P("dp"),
    )
    return jax.shard_map(
        shards,
        mesh=mesh,
        in_specs=placed,
        out_specs=(P(None, "mp"), P("mp", None), P("dp", None, "mp")),
        check_vma=False,
    )
```

profile of v0, /device:TPU:0, one launch (start us, length us, event | category | flops | bytes accessed | tf_op | source)
XLA Modules:
  0.0 227.9 jit_solution(15444329244682934595)
XLA Ops:
  7.2 0.7 all-gather.2.cloned.1.call-update
  8.0 0.9 reduce_window_sum.11
  8.8 0.7 sub.52
  9.6 0.8 select_reduce_fusion.2
  10.6 1.5 fusion.36
  14.8 0.8 reduce_sum.46
  15.6 0.8 convert_divide_fusion
  16.5 1.3 fusion.35
  17.9 0.1 copy.38
  18.4 0.8 gather_fusion
  19.2 25.8 %all-gather.2.cloned.1.call-done = bf16[128,5120]{1,0:T(8,128)(2,1)} async-done(((bf16[32,5120]{1,0:T(8,128)(2,1)}), bf16[128,5120]{1,0:T(8,128)(2,1)}) %all-gather.2.cloned.1.call-update) | async-done | bytes 1310736 | tf_op jit(solution)/shard_map/all_gather | solution.py:45
  45.0 9.6 %fusion.8 = f32[512,5120]{1,0:T(8,128)} fusion(bf16[128,5120]{1,0:T(8,128)(2,1)} %all-gather.2.cloned.1.call-done, bf16[5120,512]{1,0:T(8,128)(2,1)} %param.14, bf16[128,512]{1,0:T(8,128)(2,1)S(1)} %gather_fusion, f32[128]{0:T(128)S(1)} %mul.70, pred[128]{0:T(512)(128)(4,1)S(1)} %compare_and_fusion), kind=kOutput, calls=%fused_computation.14 | convolution fusion | flops 1342636032 | bytes 17171072 | tf_op jit(solution)/shard_map/nd,nc->dc/dot_general | solution.py:33
  54.6 4.0 %copy.40 = f32[5120,512]{0,1:T(8,128)S(1)} copy(f32[5120,512]{0,1:T(8,128)} %bitcast.57) | data formatting | bytes 20971520
  58.7 1.0 fusion.12
  59.9 4.0 %copy-done.1 = f32[5120,512]{0,1:T(8,128)} copy-done((f32[5120,512]{0,1:T(8,128)}, f32[5120,512]{0,1:T(8,128)S(1)}, u32[]{:S(2)}) %copy-start.1) | copy-done | bytes 10485784
  63.9 8.0 %fusion.37 = f32[5120,64]{0,1:T(8,128)} fusion(f32[5120,512]{0,1:T(8,128)S(1)} %fusion.9, f32[512,64]{0,1:T(8,128)S(1)} %copy-done.4), kind=kOutput, calls=%fused_computation.70 | convolution fusion | flops 2013265920 | bytes 11927552 | tf_op jit(solution)/shard_map/dot_general | solution.py:52
  72.0 0.2 all-reduce.5.cloned.1.call-start
  72.2 56.7 %all-reduce.3.cloned.1.call-done = f32[5120,64]{0,1:T(8,128)} async-done(((f32[5120,64]{0,1:T(8,128)}), f32[5120,64]{0,1:T(8,128)}) %all-reduce.3.cloned.1.call-update) | async-done | bytes 1310736 | tf_op jit(solution)/shard_map/psum | solution.py:53
  128.9 2.9 %fusion.38 = f32[64,64]{1,0:T(8,128)S(1)} fusion(f32[5120,64]{0,1:T(8,128)} %all-reduce.3.cloned.1.call-done), kind=kOutput, calls=%fused_computation.71 | convolution fusion | flops 251658240 | bytes 1327104 | tf_op jit(solution)/shard_map/dr,ds->rs/dot_general | solution.py:54
  131.9 5.8 %cholesky.16 = f32[64,64]{1,0:T(8,128)S(1)} custom-call(f32[64,64]{1,0:T(8,128)S(1)} %fusion.23), custom_call_target="Cholesky" | custom-call | tf_op jit(solution)/shard_map/jit(cholesky)/cholesky | solution.py:55
  137.7 0.6 compare_reduce_fusion
  138.4 0.7 fusion.20
  139.0 4.9 %custom-call.7 = f32[1,64,64]{1,2,0:T(8,128)S(1)} custom-call(f32[1,64,64]{2,1,0:T(8,128)S(1)} %fusion.20), custom_call_target="InvertDiagBlocksLowerTriangular" | custom-call | tf_op jit(solution)/shard_map/jit(_solve_triangular)/triangular_solve | solution.py:56
  143.9 2.6 %fusion.21 = f32[64,5120]{1,0:T(8,128)S(1)} fusion(f32[5120,64]{0,1:T(8,128)} %all-reduce.3.cloned.1.call-done, f32[1,64,64]{1,2,0:T(8,128)S(1)} %custom-call.7), kind=kOutput, calls=%fused_computation.34 | convolution fusion | flops 251658240 | bytes 2637824 | tf_op jit(solution)/shard_map/jit(_solve_triangular)/triangular_solve | solution.py:56
  146.5 13.9 %fusion.39 = f32[512,64]{0,1:T(8,128)} fusion(f32[5120,512]{0,1:T(8,128)} %copy-done.1, f32[64,5120]{1,0:T(8,128)S(1)} %fusion.21), kind=kOutput, calls=%fused_computation.72 | convolution fusion | flops 2013265920 | bytes 11927552 | tf_op jit(solution)/shard_map/dc,dr->cr/dot_general | solution.py:57
  160.5 52.3 %all-reduce.5.cloned.1.call-done = f32[512,64]{0,1:T(8,128)} async-done(((f32[512,64]{0,1:T(8,128)}), f32[512,64]{0,1:T(8,128)}) %all-reduce.5.cloned.1.call-update) | async-done | bytes 131088 | tf_op jit(solution)/shard_map/psum | solution.py:58
  212.7 0.9 broadcast_multiply_fusion
  213.7 1.6 fusion
  215.3 1.6 fusion.1
  216.8 1.6 fusion.2
  218.4 1.6 fusion.3
  220.1 1.3 copy.31
  (35 shorter events, 1.5 us)
Async XLA Ops:
  7.2 11.2 %copy-start = (bf16[256,512]{1,0:T(8,128)(2,1)S(1)}, bf16[256,512]{1,0:T(8,128)(2,1)}, u32[]{:S(2)}) copy-start(bf16[256,512]{1,0:T(8,128)(2,1)} %param.13) | copy-start | bytes 786436
  7.2 37.8 %all-gather.2.cloned.1.call-start = ((), (), s32[]{:S(2)}) async-start(), calls=%async_computation | async-start | bytes 1638400 | tf_op jit(solution)/shard_map/all_gather | solution.py:45
  7.9 120.9 %all-reduce.3.cloned.1.call-start = ((), (), s32[]{:S(2)}) async-start(), calls=%async_computation.1 | async-start | bytes 2621440 | tf_op jit(solution)/shard_map/psum | solution.py:53
  54.6 9.2 %copy-start.4 = (f32[512,64]{0,1:T(8,128)S(1)}, f32[512,64]{0,1:T(8,128)}, u32[]{:S(2)}) copy-start(f32[512,64]{0,1:T(8,128)} %param.15) | copy-start | bytes 393220
  59.9 4.0 %copy-start.1 = (f32[5120,512]{0,1:T(8,128)}, f32[5120,512]{0,1:T(8,128)S(1)}, u32[]{:S(2)}) copy-start(f32[5120,512]{0,1:T(8,128)S(1)} %fusion.9) | copy-start | bytes 31457284
  72.0 140.8 %all-reduce.5.cloned.1.call-start = ((), (), s32[]{:S(2)}) async-start(), calls=%async_computation.2 | async-start | bytes 262144 | tf_op jit(solution)/shard_map/psum | solution.py:58
  146.5 71.9 %copy-start.2 = (f32[64,5120]{1,0:T(8,128)}, f32[64,5120]{1,0:T(8,128)S(1)}, u32[]{:S(2)}) copy-start(f32[64,5120]{1,0:T(8,128)S(1)} %fusion.21) | copy-start | bytes 3932164
  213.7 7.7 %copy-start.3 = (f32[512,64]{0,1:T(8,128)}, f32[512,64]{0,1:T(8,128)S(1)}, u32[]{:S(2)}) copy-start(f32[512,64]{0,1:T(8,128)S(1)} %broadcast_multiply_fusion) | copy-start | bytes 393220
Sparse Core Ops, SparseCore 0:
  9.6 35.3 all-gather.1
  72.1 56.7 all-reduce.2
  160.6 52.1 all-reduce.4
where the time goes:
time: 228 us
  waiting for transfers between devices  135 us (59%)
  matrix products  43.3 us (19%)
  other arithmetic  18.4 us (8%)
  between operations  16.7 us (7%)
  local copies, waits for them, and re-layouts  13.7 us (6%)
    psum x1, waiting for transfers between devices, shards(): p_sum = lax.psum(p_local, 'dp')  56.7 us
    psum x1, waiting for transfers between devices, shards(): q_factor = lax.psum(q_local, 'dp') / lax.axis_size('dp')  52.3 us
    all_gather x1, waiting for transfers between devices, shards(): lax.all_gather(gen_rows, 'mp', axis=0, tiled=True)  25.8 us
    dot_general x1, matrix products, shards(): jnp.einsum('dc,dr->cr', gradient, p_factor, precision=HIGHEST_PRECISION)  13.9 us
    unnamed x16, local copies, waits for them, and re-layouts  9.83 us
    dot_general x1, matrix products, row_gradient(): jnp.einsum('nd,nc->dc', row_block, grad_h, preferred_element_type=jnp.flo...  9.64 us
    dot_general x1, matrix products, shards(): p_local = jnp.dot(gradient, q_init, precision=HIGHEST_PRECISION)  8.05 us
    another operation x3, other arithmetic, shards(): factor_low = jnp.linalg.cholesky(gram_matrix)  6.52 us
  transfers between devices with their start and end apart: 3, of which 3 were waited for; matrix products, arithmetic and copies ran while one was open for 4% of the time, Pallas kernels for 0%

commit v1 on v0

--- a/solution.py
+++ b/solution.py
@@ -4,6 +4,13 @@
 from jax.sharding import PartitionSpec as P
 
 HIGHEST_PRECISION = lax.Precision.HIGHEST
+
+
+def marks_close(target, dimension_no):
+    main = list(target.shape[1:])
+    main[dimension_no] *= target.shape[0]
+    part_next = jnp.moveaxis(target, 0, dimension_no).reshape(main)
+    return part_next
 
 
 def packed_tables(lengths, assign, rewards, slot_count, capacity):
@@ -41,9 +48,28 @@
     flat_slot = slot_table.reshape(-1)
     flat_weight = row_weight.reshape(-1)
     upstream_rows = jnp.take(upstream, flat_slot, axis=0)
-    gradient = row_gradient(
-        lax.all_gather(gen_rows, "mp", axis=0, tiled=True), upstream_rows, flat_weight, weight
-    )
+
+    def raise_ratios(w_in, across, which_dim=0):
+        how_many = lax.axis_size(across)
+        queue = list(map(lambda i: (i, (i + 1) % how_many), range(how_many)))
+        sides = [(hop_no, pp) for pp, hop_no in queue]
+        small, t1 = ([], [])
+        dev_i = 0
+        while dev_i < how_many - 1:
+            if dev_i % 2 == 0:
+                small.append(
+                    lax.ppermute(small[-1] if small else w_in, axis_name=across, perm=queue)
+                )
+            else:
+                t1.append(lax.ppermute(t1[-1] if t1 else w_in, across, perm=sides))
+            dev_i += 1
+        k_now = jnp.stack([*small[::-1], w_in, *t1], 0)
+        state_next = lax.axis_index(across) - len(small)
+        k_now = k_now[(jnp.arange(how_many) - state_next) % how_many]
+        current_value = marks_close(k_now, which_dim)
+        return current_value
+
+    gradient = row_gradient(raise_ratios(gen_rows, "mp"), upstream_rows, flat_weight, weight)
     block_rows = resid.shape[1]
     for block in range(resid.shape[0]):
         first_row = block_ids[block] * block_rows

time: 228 us -> 216 us (0.947)
  waiting for transfers between devices: 135 us -> 122 us
  local copies, waits for them, and re-layouts: 13.7 us -> 3.33 us
  other arithmetic: 18.4 us -> 25.2 us
  starting transfers between devices: 0.3 us -> 5.48 us
    all_gather x1 -> x0, waiting for transfers between devices: 25.8 us -> none  [shards(): lax.all_gather(gen_rows, 'mp', axis=0, tiled=True)]
    ppermute x0 -> x3, waiting for transfers between devices: none -> 12.4 us  [the longest x2 7.41 us: raise_ratios(): lax.ppermute(small[-1] if small else w_in, axis_name=across, perm=queue)]
    unnamed x16 -> x14, local copies, waits for them, and re-layouts: 9.83 us -> 0.05 us
    dot_general x1, matrix products: 8.05 us -> 13.9 us  [shards(): p_local = jnp.dot(gradient, q_init, precision=HIGHEST_PRECISION)]
    dynamic_update_slice x4, other arithmetic: 1.2 us -> 6.82 us  [shards(): lax.dynamic_update_slice_in_dim(gradient, current + resid[block], first_r...]
    ppermute x0 -> x3, starting transfers between devices: none -> 5.23 us  [the longest x2 3.13 us: raise_ratios(): lax.ppermute(small[-1] if small else w_in, axis_name=across, perm=queue)]
    dot_general x1, matrix products: 13.9 us -> 10.6 us  [shards(): jnp.einsum('dc,dr->cr', gradient, p_factor, precision=HIGHEST_PRECISION)]
  transfers between devices with their start and end apart: 3 -> 5, of which waited for: 3 -> 4; matrix products, arithmetic and copies ran while one was open for 4% -> 3% of each run, Pallas kernels for 0% -> 0%
where the time goes in v1:
time: 216 us
  waiting for transfers between devices  122 us (56%)
  matrix products  43.2 us (20%)
  other arithmetic  25.2 us (12%)
  between operations  16.9 us (8%)
  starting transfers between devices  5.48 us (3%)
  local copies, waits for them, and re-layouts  3.33 us (2%)
    psum x1, waiting for transfers between devices, shards(): p_sum = lax.psum(p_local, 'dp')  56.9 us
    psum x1, waiting for transfers between devices, shards(): q_factor = lax.psum(q_local, 'dp') / lax.axis_size('dp')  52.3 us
    dot_general x1, matrix products, shards(): p_local = jnp.dot(gradient, q_init, precision=HIGHEST_PRECISION)  13.9 us
    dot_general x1, matrix products, shards(): jnp.einsum('dc,dr->cr', gradient, p_factor, precision=HIGHEST_PRECISION)  10.6 us
    dot_general x1, matrix products, row_gradient(): jnp.einsum('nd,nc->dc', row_block, grad_h, preferred_element_type=jnp.flo...  8.93 us
    ppermute x2, waiting for transfers between devices, raise_ratios(): lax.ppermute(small[-1] if small else w_in, axis_name=across, perm=queue)  7.41 us
    dynamic_update_slice x4, other arithmetic, shards(): lax.dynamic_update_slice_in_dim(gradient, current + resid[block], first_r...  6.82 us
    another operation x3, other arithmetic, shards(): factor_low = jnp.linalg.cholesky(gram_matrix)  6.52 us
  transfers between devices with their start and end apart: 5, of which 4 were waited for; matrix products, arithmetic and copies ran while one was open for 3% of the time, Pallas kernels for 0%

profile of v1, /device:TPU:0, one launch (start us, length us, event | category | flops | bytes accessed | tf_op | source)
XLA Modules:
  0.0 215.8 jit_solution(9984109470992102343)
XLA Ops:
  7.2 3.1 %collective-permute-start = (bf16[32,5120]{1,0:T(8,128)(2,1)}, bf16[32,5120]{1,0:T(8,128)(2,1)S(1)}, u32[]{:S(2)}, u32[]{:S(2)}) collective-permute-start(bf16[32,5120]{1,0:T(8,128)(2,1)} %param.9), channel_id=1, source_target_pairs={{0,1},{1,2},{2,3},{3,0},{4,5},{5,6},{6,7},{7,4},{8,9},{9,10},{10,1... | collective-permute-start | bytes 983048 | tf_op jit(solution)/shard_map/ppermute | solution.py:61
  10.3 2.1 collective-permute-start.2
  12.4 0.9 reduce_window_sum.11
  13.3 0.7 sub.71
  14.0 0.8 select_reduce_fusion.2
  15.1 1.5 fusion.37
  19.2 0.8 reduce_sum.46
  20.0 0.8 convert_divide_fusion
  20.9 0.8 gather_fusion.1
  21.9 5.0 %collective-permute-done.2 = bf16[32,5120]{1,0:T(8,128)(2,1)S(1)} collective-permute-done((bf16[32,5120]{1,0:T(8,128)(2,1)}, bf16[32,5120]{1,0:T(8,128)(2,1)S(1)}, u32[]{:S(2)}, u32[]{:S(2)}) %collective-permute-start.2) | collective-permute-done | bytes 327712 | tf_op jit(solution)/shard_map/ppermute | solution.py:64
  26.9 7.4 %collective-permute-done.1 = bf16[32,5120]{1,0:T(8,128)(2,1)S(1)} collective-permute-done((bf16[32,5120]{1,0:T(8,128)(2,1)S(1)}, bf16[32,5120]{1,0:T(8,128)(2,1)S(1)}, u32[]{:S(2)}, u32[]{:S(2)}) %collective-permute-start.1) | collective-permute-done | bytes 327712 | tf_op jit(solution)/shard_map/ppermute | solution.py:61
  35.2 8.9 %fusion.8 = f32[5120,512]{1,0:T(8,128)} fusion(bf16[128,5120]{1,0:T(8,128)(2,1)S(1)} %bitcast.61, bf16[5120,512]{1,0:T(8,128)(2,1)} %param.14, bf16[128,512]{1,0:T(8,128)(2,1)S(1)} %gather_fusion.1, f32[128]{0:T(128)S(1)} %mul.70, pred[128]{0:T(512)(128)(4,1)S(1)} %compare_and_fusion), kind=kOutput, calls=%fused_computation.16 | convolution fusion | flops 1342636032 | bytes 17171072 | tf_op jit(solution)/shard_map/nd,nc->dc/dot_general | solution.py:40
  44.1 1.7 fusion.12
  45.8 1.7 fusion.11
  47.5 1.7 fusion.10
  49.2 1.7 fusion.9
  50.9 13.9 %fusion.38 = f32[5120,64]{0,1:T(8,128)} fusion(f32[5120,512]{1,0:T(8,128)} %fusion.9, f32[512,64]{0,1:T(8,128)S(1)} %copy-done.6), kind=kOutput, calls=%fused_computation.78 | convolution fusion | flops 2013265920 | bytes 11927552 | tf_op jit(solution)/shard_map/dot_general | solution.py:78
  65.1 56.9 %all-reduce.3.cloned.1.call-done = f32[5120,64]{0,1:T(8,128)} async-done(((f32[5120,64]{0,1:T(8,128)}), f32[5120,64]{0,1:T(8,128)}) %all-reduce.3.cloned.1.call-update) | async-done | bytes 1310736 | tf_op jit(solution)/shard_map/psum | solution.py:79
  122.0 3.0 %fusion.39 = f32[64,64]{1,0:T(8,128)S(1)} fusion(f32[5120,64]{0,1:T(8,128)} %all-reduce.3.cloned.1.call-done), kind=kOutput, calls=%fused_computation.79 | convolution fusion | flops 251658240 | bytes 1327104 | tf_op jit(solution)/shard_map/dr,ds->rs/dot_general | solution.py:80
  125.1 5.8 %cholesky.16 = f32[64,64]{1,0:T(8,128)S(1)} custom-call(f32[64,64]{1,0:T(8,128)S(1)} %fusion.23), custom_call_target="Cholesky" | custom-call | tf_op jit(solution)/shard_map/jit(cholesky)/cholesky | solution.py:81
  131.0 0.6 compare_reduce_fusion
  131.7 0.7 fusion.20
  132.3 4.9 %custom-call.7 = f32[1,64,64]{1,2,0:T(8,128)S(1)} custom-call(f32[1,64,64]{2,1,0:T(8,128)S(1)} %fusion.20), custom_call_target="InvertDiagBlocksLowerTriangular" | custom-call | tf_op jit(solution)/shard_map/jit(_solve_triangular)/triangular_solve | solution.py:82
  137.2 1.2 fusion.21
  138.5 10.6 %fusion.40 = f32[512,64]{0,1:T(8,128)} fusion(f32[5120,512]{1,0:T(8,128)} %fusion.9, f32[64,5120]{1,0:T(8,128)S(1)} %fusion.21), kind=kOutput, calls=%fused_computation.80 | convolution fusion | flops 2013265920 | bytes 11927552 | tf_op jit(solution)/shard_map/dc,dr->cr/dot_general | solution.py:83
  149.1 52.3 %all-reduce.5.cloned.1.call-done = f32[512,64]{0,1:T(8,128)} async-done(((f32[512,64]{0,1:T(8,128)}), f32[512,64]{0,1:T(8,128)}) %all-reduce.5.cloned.1.call-update) | async-done | bytes 131088 | tf_op jit(solution)/shard_map/psum | solution.py:84
  201.4 0.9 broadcast_multiply_fusion
  202.3 1.4 fusion
  203.8 1.4 fusion.1
  205.2 1.4 fusion.2
  206.6 1.4 fusion.3
  207.9 1.0 pad_maximum_fusion.1
  (39 shorter events, 1.9 us)
Async XLA Ops:
  7.2 13.8 %copy-start = (bf16[256,512]{1,0:T(8,128)(2,1)S(1)}, bf16[256,512]{1,0:T(8,128)(2,1)}, u32[]{:S(2)}) copy-start(bf16[256,512]{1,0:T(8,128)(2,1)} %param.13) | copy-start | bytes 786436
  7.2 27.2 %copy-start.5 = (bf16[32,5120]{1,0:T(8,128)(2,1)S(1)}, bf16[32,5120]{1,0:T(8,128)(2,1)}, u32[]{:S(2)}) copy-start(bf16[32,5120]{1,0:T(8,128)(2,1)} %param.9) | copy-start | bytes 983044
  7.2 114.8 %all-reduce.3.cloned.1.call-start = ((), (), s32[]{:S(2)}) async-start(), calls=%async_computation | async-start | bytes 2621440 | tf_op jit(solution)/shard_map/psum | solution.py:79
  7.2 14.6 %collective-permute-start = (bf16[32,5120]{1,0:T(8,128)(2,1)}, bf16[32,5120]{1,0:T(8,128)(2,1)S(1)}, u32[]{:S(2)}, u32[]{:S(2)}) collective-permute-start(bf16[32,5120]{1,0:T(8,128)(2,1)} %param.9), channel_id=1, source_target_pairs={{0,1},{1,2},{2,3},{3,0},{4,5},{5,6},{6,7},{7,4},{8,9},{9,10},{10,1... | collective-permute-start | bytes 983048 | tf_op jit(solution)/shard_map/ppermute | solution.py:61
  10.3 16.6 %collective-permute-start.2 = (bf16[32,5120]{1,0:T(8,128)(2,1)}, bf16[32,5120]{1,0:T(8,128)(2,1)S(1)}, u32[]{:S(2)}, u32[]{:S(2)}) collective-permute-start(bf16[32,5120]{1,0:T(8,128)(2,1)} %param.9), channel_id=1, source_target_pairs={{1,0},{2,1},{3,2},{0,3},{5,4},{6,5},{7,6},{4,7},{9,8},{10,9},{11,1... | collective-permute-start | bytes 983048 | tf_op jit(solution)/shard_map/ppermute | solution.py:64
  21.8 12.5 %collective-permute-start.1 = (bf16[32,5120]{1,0:T(8,128)(2,1)S(1)}, bf16[32,5120]{1,0:T(8,128)(2,1)S(1)}, u32[]{:S(2)}, u32[]{:S(2)}) collective-permute-start(bf16[32,5120]{1,0:T(8,128)(2,1)S(1)} %collective-permute-done), channel_id=1, source_target_pairs={{0,1},{1,2},{2,3},{3,0},{4,5},{5,6},{6,7},{7,4},{8,9},{9,10},{10,1... | collective-permute-start | bytes 983048 | tf_op jit(solution)/shard_map/ppermute | solution.py:61
  35.2 8.9 %copy-start.4 = (f32[4,128,512]{2,1,0:T(8,128)S(1)}, f32[4,128,512]{2,1,0:T(8,128)}, u32[]{:S(2)}) copy-start(f32[4,128,512]{2,1,0:T(8,128)} %param.16) | copy-start | bytes 3145732
  45.8 5.1 %copy-start.6 = (f32[512,64]{0,1:T(8,128)S(1)}, f32[512,64]{0,1:T(8,128)}, u32[]{:S(2)}) copy-start(f32[512,64]{0,1:T(8,128)} %param.15) | copy-start | bytes 393220
  64.8 136.6 %all-reduce.5.cloned.1.call-start = ((), (), s32[]{:S(2)}) async-start(), calls=%async_computation.1 | async-start | bytes 262144 | tf_op jit(solution)/shard_map/psum | solution.py:84
  122.0 15.2 %copy-start.1 = (f32[5120,64]{0,1:T(8,128)S(1)}, f32[5120,64]{0,1:T(8,128)}, u32[]{:S(2)}) copy-start(f32[5120,64]{0,1:T(8,128)} %all-reduce.3.cloned.1.call-done) | copy-start | bytes 3932164
  138.5 68.1 %copy-start.2 = (f32[64,5120]{1,0:T(8,128)}, f32[64,5120]{1,0:T(8,128)S(1)}, u32[]{:S(2)}) copy-start(f32[64,5120]{1,0:T(8,128)S(1)} %fusion.21) | copy-start | bytes 3932164
  202.3 5.6 %copy-start.3 = (f32[512,64]{0,1:T(8,128)}, f32[512,64]{0,1:T(8,128)S(1)}, u32[]{:S(2)}) copy-start(f32[512,64]{0,1:T(8,128)S(1)} %broadcast_multiply_fusion) | copy-start | bytes 393220
Sparse Core Ops, SparseCore 0:
  65.0 57.0 all-reduce.2
  149.2 52.1 all-reduce.4
